TPU v7x, 32 devices: a whole 2x2x4 slice. The times are simulated.
32 devices in a mesh: row: 8 (over y, x, core), col: 4 (over z).
Axes of the slice: x: 2, y: 2, z: 4, core: 2. Of those that a mesh axis runs over, the one named last changes fastest.
Arguments:
- right_sides: float32 [64, 32768], P(None, ('row', 'col'))
- diag_tiles: float32 [32, 1024, 1024], P(('row', 'col')), as said below
- low_rank: float32 [32, 4, 8, 2, 12, 1024], P('row', 'col'), as said below
- tile_ranks: int32 [32, 4, 8], P('row', 'col'), may hold values from 1 to 12, as said below
- inv_factor: float32 [256, 8, 128, 128], P(('row', 'col')), as said below
- sub_sizes: int32 [64], replicated, may hold values from 1 to 8, 256 in all
Outputs:
- solution: float32 [64, 32768], P(None, ('row', 'col'))
- residual: float32 [64, 32768], P(None, ('row', 'col'))
Inputs may be any that keep to these rules, and one draw needn't show every extreme that they name: `low_rank`: tile (j, i) holds the two factors of tile (i, j) in swapped order, and a diagonal tile's two factors are equal, so S is symmetric. `tile_ranks`: the rank of tile (i, j) equals that of tile (j, i); diagonal tiles have rank 12. `diag_tiles`: each tile is symmetric positive definite. `inv_factor`: the block at distance 0 of every span is lower triangular with a positive diagonal. `sub_sizes`: the sizes sum to 256.
All inputs are finite; a program needn't handle non-finite values.
Results may differ from a plain program's by a relative error of at most 0.0003.
Values sent between devices are 32-bit elements; how exact they have to be, the bound alone decides.
A program may use at most 128 MiB of HBM per device.

v0:
```python
import jax
import jax.numpy as jnp
from jax import lax
from jax.sharding import PartitionSpec as P

RANK = 12
finest = lax.Precision.HIGHEST


def shifted(x, axis, by):
    size = lax.axis_size(axis)
    pairs = [(i, i + by) for i in range(size) if 0 <= i + by < size]
    return lax.ppermute(x, axis, pairs)


def span_weights(sub_sizes, per_device, reach_len):
    span_ids = lax.axis_index(("row", "col")) * per_device + lax.iota(jnp.int32, per_device)
    ending = jnp.cumsum(sub_sizes)
    opening = ending - sub_sizes
    inside = (span_ids[:, None] >= opening[None, :]) & (span_ids[:, None] < ending[None, :])
    position = span_ids - jnp.sum(jnp.where(inside, opening[None, :], 0), axis=1)
    return (lax.iota(jnp.int32, reach_len)[None, :] <= position[:, None]).astype(jnp.float32)


def precondition(vector, inv_factor, weights):
    rhs_count, tile_len = vector.shape
    per_device = inv_factor.shape[0]
    reach_len = inv_factor.shape[1]
    span_len = inv_factor.shape[2]
    before = shifted(vector, ("row", "col"), 1)
    joined = jnp.concatenate([before, vector], axis=1).reshape(rhs_count, 2 * per_device, span_len)
    windows = jnp.stack(
        [joined[:, per_device - behind : 2 * per_device - behind] for behind in range(reach_len)],
        axis=2,
    )
    windows = windows * weights[None, :, :, None]
    forward = jnp.einsum("ltji,klti->klj", inv_factor, windows, precision=finest)
    spread = (
        jnp.einsum("ltji,klj->klti", inv_factor, forward, precision=finest)
        * weights[None, :, :, None]
    )
    placed = jnp.zeros_like(joined)
    for behind in range(reach_len):
        placed = placed + jnp.pad(
            spread[:, :, behind], ((0, 0), (per_device - behind, behind), (0, 0))
        )
    returned = shifted(placed[:, :per_device].reshape(rhs_count, tile_len), ("row", "col"), -1)
    return placed[:, per_device:].reshape(rhs_count, tile_len) + returned


def operate(vector, diag_tiles, low_rank, tile_ranks):
    rhs_count, tile_len = vector.shape
    tile_rows = low_rank.shape[0]
    local_part = jnp.dot(vector, diag_tiles[0], precision=finest)
    left_factor = low_rank[:, 0, :, 0]
    right_factor = low_rank[:, 0, :, 1]
    weights = (lax.iota(jnp.int32, RANK)[None, None, :] < tile_ranks[:, 0, :, None]).astype(
        jnp.float32
    )
    initial = jnp.zeros((rhs_count, tile_rows * tile_len), jnp.float32)
    piece = lax.all_gather(vector, "row", axis=1, tiled=True)
    count_tiles = piece.shape[1] // tile_len
    pieces = piece.reshape(rhs_count, count_tiles, tile_len)
    coeffs = (
        jnp.einsum("bmqt,pmt->bmqp", right_factor, pieces, precision=finest)
        * weights[:, :, :, None]
    )
    added = jnp.einsum("bmqt,bmqp->pbt", left_factor, coeffs, precision=finest)
    partial_rows = initial + added.reshape(rhs_count, tile_rows * tile_len)
    summed = lax.psum_scatter(partial_rows, "col", scatter_dimension=1, tiled=True)
    return local_part + summed


def solve_spd(matrix, target):
    factor = jnp.linalg.cholesky(matrix)
    return jax.scipy.linalg.cho_solve((factor, True), target)


def gram_of(first_block, second_block):
    return jnp.dot(first_block, second_block.T, precision=finest)


def apply_coeffs(coeffs, block_rows):
    return jnp.dot(coeffs.T, block_rows, precision=finest)


def global_sum(terms):
    return lax.psum((terms[0], terms[1]), ("row", "col"))


def body(right_sides, diag_tiles, low_rank, tile_ranks, inv_factor, sub_sizes):
    weights = span_weights(sub_sizes, inv_factor.shape[0], inv_factor.shape[1])
    residual = right_sides
    search = precondition(residual, inv_factor, weights)
    images = operate(search, diag_tiles, low_rank, tile_ranks)
    rho_now, curvature = global_sum((gram_of(search, residual), gram_of(search, images)))
    step_size = solve_spd(curvature, rho_now)
    solution = apply_coeffs(step_size, search)
    residual = residual - apply_coeffs(step_size, images)
    precond = precondition(residual, inv_factor, weights)
    product = operate(precond, diag_tiles, low_rank, tile_ranks)
    rho_next, self_term, cross_term = lax.psum(
        (gram_of(precond, residual), gram_of(precond, product), gram_of(search, product)),
        ("row", "col"),
    )
    beta_mix = solve_spd(rho_now, rho_next)
    curvature = (
        self_term
        + jnp.dot(cross_term.T, beta_mix, precision=finest)
        + jnp.dot(beta_mix.T, cross_term, precision=finest)
        + jnp.dot(beta_mix.T, jnp.dot(curvature, beta_mix, precision=finest), precision=finest)
    )
    search = precond + apply_coeffs(beta_mix, search)
    images = product + apply_coeffs(beta_mix, images)
    step_size = solve_spd(curvature, rho_next)
    solution = solution + apply_coeffs(step_size, search)
    residual = residual - apply_coeffs(step_size, images)
    return (solution, residual)


def solution(mesh):
    placed = (
        P(None, ("row", "col")),
        P(("row", "col"), None, None),
        P("row", "col", None, None, None, None),
        P("row", "col", None),
        P(("row", "col"), None, None, None),
        P(),
    )
    return jax.shard_map(
        body,
        mesh=mesh,
        in_specs=placed,
        out_specs=(P(None, ("row", "col")), P(None, ("row", "col"))),
        check_vma=False,
    )
```

profile of v0, /device:TPU:0, one launch (start us, length us, event | category | flops | bytes accessed | tf_op | source)
XLA Modules:
  0.0 335.0 jit_solution(9789738542311892284)
XLA Ops:
  7.2 5.0 %collective-permute-start = (f32[64,1024]{1,0:T(8,128)}, f32[64,1024]{1,0:T(8,128)S(1)}, u32[]{:S(2)}, u32[]{:S(2)}) collective-permute-start(f32[64,1024]{1,0:T(8,128)} %param.9), channel_id=1, source_target_pairs={{0,1},{1,2},{2,3},{3,4},{4,5},{5,6},{6,7},{7,8},{8,9},{9,10},{10,1... | collective-permute-start | bytes 786440 | tf_op jit(solution)/shard_map/ppermute | solution.py:13
  14.1 3.9 %collective-permute-done = f32[64,1024]{1,0:T(8,128)S(1)} collective-permute-done((f32[64,1024]{1,0:T(8,128)}, f32[64,1024]{1,0:T(8,128)S(1)}, u32[]{:S(2)}, u32[]{:S(2)}) %collective-permute-start) | collective-permute-done | bytes 262176 | tf_op jit(solution)/shard_map/ppermute | solution.py:13
  21.5 4.6 %fusion.20 = f32[64,8,128,1]{2,0,3,1:T(8,128)S(1)} fusion(f32[8,8,128,128]{3,2,1,0:T(8,128)S(1)} %copy-done, f32[64,8,8,128]{3,0,2,1:T(8,128)S(1)} %fusion.62, f32[8,8]{1,0:T(8,128)S(1)} %fusion.89), kind=kOutput, calls=%fused_computation.23 | convolution fusion | flops 805830656 | bytes 6553856 | tf_op jit(solution)/shard_map/ltji,klti->klj/dot_general | solution.py:37
  30.3 8.7 %collective-permute-done.1 = f32[64,1024]{1,0:T(8,128)S(1)} collective-permute-done((f32[64,1024]{1,0:T(8,128)S(1)}, f32[64,1024]{1,0:T(8,128)S(1)}, u32[]{:S(2)}, u32[]{:S(2)}) %collective-permute-start.1) | collective-permute-done | bytes 262176 | tf_op jit(solution)/shard_map/ppermute | solution.py:13
  40.5 6.1 %fusion.91 = (f32[4,1,8,1,12,1024]{5,3,4,2,1,0:T(1,128)S(1)}, f32[4,1,8,1,12,1024]{5,3,4,2,1,0:T(1,128)S(1)}) fusion(f32[4,1,8,2,12,1024]{5,3,4,2,1,0:T(2,128)} %param.11), kind=kLoop, calls=%fused_computation.139 | loop fusion | bytes 6291456 | tf_op jit(solution)/shard_map/slice | solution.py:55
  46.6 25.1 %all-gather.3.cloned.1.call-done = f32[64,8192]{1,0:T(8,128)} async-done(((f32[64,1024]{1,0:T(8,128)}), f32[64,8192]{1,0:T(8,128)}) %all-gather.3.cloned.1.call-update) | async-done | bytes 2097168 | tf_op jit(solution)/shard_map/all_gather | solution.py:61
  82.3 25.9 %reduce-scatter.3.cloned.1.call-done = f32[64,1024]{1,0:T(8,128)} async-done(((f32[64,4096]{1,0:T(8,128)}), f32[64,1024]{1,0:T(8,128)}) %reduce-scatter.3.cloned.1.call-update) | async-done | bytes 262160 | tf_op jit(solution)/shard_map/reduce_scatter | solution.py:70
  108.2 4.9 %fusion.26 = f32[64,1024]{1,0:T(8,128)S(1)} fusion(f32[64,1024]{1,0:T(8,128)} %reduce-scatter.3.cloned.1.call-done, f32[64,1024]{1,0:T(8,128)S(1)} %copy-done.2, f32[1,1024,1024]{2,1,0:T(8,128)} %param.10), kind=kOutput, calls=%fused_computation.25 | convolution fusion | flops 805371904 | bytes 4980736 | tf_op jit(solution)/shard_map/dot_general | solution.py:54
  114.1 39.2 %all-reduce.17 = (f32[64,64]{0,1:T(8,128)S(1)}, f32[64,64]{0,1:T(8,128)S(1)}) all-reduce(f32[64,64]{0,1:T(8,128)S(1)} %fusion.95, f32[64,64]{0,1:T(8,128)S(1)} %fusion.94), channel_id=1, replica_groups=mesh['row'=8,'col'=4] {'row','col'}, use_global_device_ids=true, to_apply=%region_6.8 | all-reduce | flops 8192 | bytes 65536 | tf_op jit(solution)/shard_map/psum | solution.py:88
  153.4 5.8 %cholesky.59 = f32[64,64]{1,0:T(8,128)S(1)} custom-call(f32[64,64]{1,0:T(8,128)S(1)} %fusion.87), custom_call_target="Cholesky" | custom-call | tf_op jit(solution)/shard_map/jit(cholesky)/cholesky | solution.py:75
  161.4 5.7 %custom-call.9 = f32[1,64,64]{1,2,0:T(8,128)S(1)} custom-call(f32[1,64,64]{2,1,0:T(8,128)} %fusion.70), custom_call_target="InvertDiagBlocksLowerTriangular" | custom-call | tf_op jit(solution)/shard_map/jit(_cho_solve)/triangular_solve | solution.py:76
  168.9 3.8 %collective-permute-start.2 = (f32[64,1024]{1,0:T(8,128)S(1)}, f32[64,1024]{1,0:T(8,128)S(1)}, u32[]{:S(2)}, u32[]{:S(2)}) collective-permute-start(f32[64,1024]{1,0:T(8,128)S(1)} %convolution_subtract_fusion.1), channel_id=1, source_target_pairs={{0,1},{1,2},{2,3},{3,4},{4,5},{5,6},{6,7},{7,8},{8,9},{9,10},{10,1... | collective-permute-start | bytes 786440 | tf_op jit(solution)/shard_map/ppermute | solution.py:13
  172.7 4.7 %collective-permute-done.2 = f32[64,1024]{1,0:T(8,128)S(1)} collective-permute-done((f32[64,1024]{1,0:T(8,128)S(1)}, f32[64,1024]{1,0:T(8,128)S(1)}, u32[]{:S(2)}, u32[]{:S(2)}) %collective-permute-start.2) | collective-permute-done | bytes 262176 | tf_op jit(solution)/shard_map/ppermute | solution.py:13
  179.9 4.6 %fusion.23 = f32[64,8,128,1]{2,0,3,1:T(8,128)S(1)} fusion(f32[8,8,128,128]{3,2,1,0:T(8,128)S(1)} %copy-done.1, f32[64,8,8,128]{3,0,2,1:T(8,128)S(1)} %fusion.54, f32[8,8]{1,0:T(8,128)S(1)} %copy-done.9), kind=kOutput, calls=%fused_computation.24 | convolution fusion | flops 805830656 | bytes 6553856 | tf_op jit(solution)/shard_map/ltji,klti->klj/dot_general | solution.py:37
  188.7 9.1 %collective-permute-done.3 = f32[64,1024]{1,0:T(8,128)S(1)} collective-permute-done((f32[64,1024]{1,0:T(8,128)S(1)}, f32[64,1024]{1,0:T(8,128)S(1)}, u32[]{:S(2)}, u32[]{:S(2)}) %collective-permute-start.3) | collective-permute-done | bytes 262176 | tf_op jit(solution)/shard_map/ppermute | solution.py:13
  198.8 29.4 %all-gather.5.cloned.1.call-done = f32[64,8192]{1,0:T(8,128)} async-done(((f32[64,1024]{1,0:T(8,128)}), f32[64,8192]{1,0:T(8,128)}) %all-gather.5.cloned.1.call-update) | async-done | bytes 2097168 | tf_op jit(solution)/shard_map/all_gather | solution.py:61
  231.0 3.6 %fusion.47 = f32[4,8,12,64]{3,2,0,1:T(8,128)S(1)} fusion(f32[4,1,8,1,12,1024]{5,3,4,2,1,0:T(1,128)S(1)} %get-tuple-element.10, f32[64,8,1024,1]{2,1,0,3:T(8,128)S(1)} %bitcast.312, f32[4,8,12]{2,0,1:T(4,128)S(1)} %fusion.88), kind=kOutput, calls=%fused_computation.35 | convolution fusion | flops 302014464 | bytes 3769856 | tf_op jit(solution)/shard_map/bmqt,pmt->bmqp/dot_general | solution.py:65
  237.4 5.8 %cholesky.70 = f32[64,64]{1,0:T(8,128)S(1)} custom-call(f32[64,64]{1,0:T(8,128)S(1)} %fusion.82), custom_call_target="Cholesky" | custom-call | tf_op jit(solution)/shard_map/jit(cholesky)/cholesky | solution.py:75
  244.6 4.9 %custom-call.10 = f32[1,64,64]{1,2,0:T(8,128)S(1)} custom-call(f32[1,64,64]{2,1,0:T(8,128)S(1)} %fusion.71), custom_call_target="InvertDiagBlocksLowerTriangular" | custom-call | tf_op jit(solution)/shard_map/jit(_cho_solve)/triangular_solve | solution.py:76
  249.9 15.0 %reduce-scatter.5.cloned.1.call-done = f32[64,1024]{1,0:T(8,128)} async-done(((f32[64,4096]{1,0:T(8,128)}), f32[64,1024]{1,0:T(8,128)}) %reduce-scatter.5.cloned.1.call-update) | async-done | bytes 262160 | tf_op jit(solution)/shard_map/reduce_scatter | solution.py:70
  264.8 4.8 %fusion.29 = f32[64,1024]{1,0:T(8,128)S(1)} fusion(f32[64,1024]{1,0:T(8,128)} %reduce-scatter.5.cloned.1.call-done, f32[64,1024]{1,0:T(8,128)S(1)} %copy-done.3, f32[1,1024,1024]{2,1,0:T(8,128)} %param.10), kind=kOutput, calls=%fused_computation.26 | convolution fusion | flops 805371904 | bytes 4980736 | tf_op jit(solution)/shard_map/dot_general | solution.py:54
  270.4 40.1 %all-reduce.16 = (f32[64,64]{1,0:T(8,128)S(1)}, f32[64,64]{1,0:T(8,128)S(1)}, f32[64,64]{0,1:T(8,128)S(1)}) all-reduce(f32[64,64]{1,0:T(8,128)S(1)} %fusion.98, f32[64,64]{1,0:T(8,128)S(1)} %fusion.97, f32[64,64]{0,1:T(8,128)S(1)} %fusion.96), channel_id=1, replica_groups=mesh['row'=8,'col'=4] {'row','col'}, use_global_device_ids=true, to_apply=%region_10.13 | all-reduce | flops 12288 | bytes 98304 | tf_op jit(solution)/shard_map/psum | solution.py:102
  312.8 5.8 %cholesky.81 = f32[64,64]{1,0:T(8,128)S(1)} custom-call(f32[64,64]{1,0:T(8,128)S(1)} %fusion.77), custom_call_target="Cholesky" | custom-call | tf_op jit(solution)/shard_map/jit(cholesky)/cholesky | solution.py:75
  320.0 4.9 %custom-call.11 = f32[1,64,64]{1,2,0:T(8,128)S(1)} custom-call(f32[1,64,64]{2,1,0:T(8,128)S(1)} %fusion.72), custom_call_target="InvertDiagBlocksLowerTriangular" | custom-call | tf_op jit(solution)/shard_map/jit(_cho_solve)/triangular_solve | solution.py:76
  (119 shorter events, 48.6 us)
Async XLA Ops:
  7.2 64.6 %all-gather.3.cloned.1.call-start = ((), (), s32[]{:S(2)}) async-start(), calls=%async_computation.2 | async-start | bytes 2359296 | tf_op jit(solution)/shard_map/all_gather | solution.py:61
  7.2 10.8 %collective-permute-start = (f32[64,1024]{1,0:T(8,128)}, f32[64,1024]{1,0:T(8,128)S(1)}, u32[]{:S(2)}, u32[]{:S(2)}) collective-permute-start(f32[64,1024]{1,0:T(8,128)} %param.9), channel_id=1, source_target_pairs={{0,1},{1,2},{2,3},{3,4},{4,5},{5,6},{6,7},{7,8},{8,9},{9,10},{10,1... | collective-permute-start | bytes 786440 | tf_op jit(solution)/shard_map/ppermute | solution.py:13
  14.1 12.0 %copy-start.8 = (f32[8,8]{1,0:T(8,128)}, f32[8,8]{1,0:T(8,128)S(1)}, u32[]{:S(2)}) copy-start(f32[8,8]{1,0:T(8,128)S(1)} %fusion.89) | copy-start | bytes 772
  19.3 2.2 copy-start
  28.7 11.6 %copy-start.10 = (s32[4,1,8]{2,1,0:T(1,128)S(1)}, s32[4,1,8]{2,1,0:T(1,128)}, u32[]{:S(2)}) copy-start(s32[4,1,8]{2,1,0:T(1,128)} %param.12) | copy-start | bytes 388
  29.0 10.0 %collective-permute-start.1 = (f32[64,1024]{1,0:T(8,128)S(1)}, f32[64,1024]{1,0:T(8,128)S(1)}, u32[]{:S(2)}, u32[]{:S(2)}) collective-permute-start(f32[64,1024]{1,0:T(8,128)S(1)} %bitcast.318), channel_id=1, source_target_pairs={{1,0},{2,1},{3,2},{4,3},{5,4},{6,5},{7,6},{8,7},{9,8},{10,9},{11,1... | collective-permute-start | bytes 786440 | tf_op jit(solution)/shard_map/ppermute | solution.py:13
  39.8 68.4 %reduce-scatter.3.cloned.1.call-start = ((), (), s32[]{:S(2)}) async-start(), calls=%async_computation.3 | async-start | bytes 1310720 | tf_op jit(solution)/shard_map/reduce_scatter | solution.py:70
  79.7 1.3 copy-start.2
  80.8 147.5 %all-gather.5.cloned.1.call-start = ((), (), s32[]{:S(2)}) async-start(), calls=%async_computation.4 | async-start | bytes 2359296 | tf_op jit(solution)/shard_map/all_gather | solution.py:61
  113.1 0.7 copy-start.4
  168.9 8.6 %copy-start.6 = (f32[64,1024]{1,0:T(8,128)}, f32[64,1024]{1,0:T(8,128)S(1)}, u32[]{:S(2)}) copy-start(f32[64,1024]{1,0:T(8,128)S(1)} %convolution_subtract_fusion.1) | copy-start | bytes 786436
  168.9 8.6 %collective-permute-start.2 = (f32[64,1024]{1,0:T(8,128)S(1)}, f32[64,1024]{1,0:T(8,128)S(1)}, u32[]{:S(2)}, u32[]{:S(2)}) collective-permute-start(f32[64,1024]{1,0:T(8,128)S(1)} %convolution_subtract_fusion.1), channel_id=1, source_target_pairs={{0,1},{1,2},{2,3},{3,4},{4,5},{5,6},{6,7},{7,8},{8,9},{9,10},{10,1... | collective-permute-start | bytes 786440 | tf_op jit(solution)/shard_map/ppermute | solution.py:13
  177.7 2.2 copy-start.1
  177.8 2.2 copy-start.9
  187.4 10.4 %collective-permute-start.3 = (f32[64,1024]{1,0:T(8,128)S(1)}, f32[64,1024]{1,0:T(8,128)S(1)}, u32[]{:S(2)}, u32[]{:S(2)}) collective-permute-start(f32[64,1024]{1,0:T(8,128)S(1)} %bitcast.319), channel_id=1, source_target_pairs={{1,0},{2,1},{3,2},{4,3},{5,4},{6,5},{7,6},{8,7},{9,8},{10,9},{11,1... | collective-permute-start | bytes 786440 | tf_op jit(solution)/shard_map/ppermute | solution.py:13
  198.6 66.3 %reduce-scatter.5.cloned.1.call-start = ((), (), s32[]{:S(2)}) async-start(), calls=%async_computation.5 | async-start | bytes 1310720 | tf_op jit(solution)/shard_map/reduce_scatter | solution.py:70
  236.2 13.3 %copy-start.3 = (f32[64,1024]{1,0:T(8,128)S(1)}, f32[64,1024]{1,0:T(8,128)}, u32[]{:S(2)}) copy-start(f32[64,1024]{1,0:T(8,128)} %bitcast_add_fusion) | copy-start | bytes 786436
  236.2 13.3 %copy-start.7 = (f32[64,1024]{1,0:T(8,128)S(1)}, f32[64,1024]{1,0:T(8,128)}, u32[]{:S(2)}) copy-start(f32[64,1024]{1,0:T(8,128)} %copy-done.6) | copy-start | bytes 786436
  249.9 61.0 %copy-start.5 = (f32[64,1024]{1,0:T(8,128)S(1)}, f32[64,1024]{1,0:T(8,128)}, u32[]{:S(2)}) copy-start(f32[64,1024]{1,0:T(8,128)} %copy-done.4) | copy-start | bytes 786436
Sparse Core Ops, SparseCore 0:
  39.9 31.7 all-gather.2
  80.9 27.2 reduce-scatter.2
  198.7 29.5 all-gather.4
  237.4 27.3 reduce-scatter.4
where the time goes:
time: 341 us; the launch traced here: 335 us
  waiting for transfers between devices  122 us (36%)
  blocking collectives  79.3 us (23%)
  matrix products  43.8 us (13%)
  other arithmetic  41.8 us (12%)
  local copies, waits for them, and re-layouts  20.9 us (6%)
  between operations  14.9 us (4%)
  starting transfers between devices  12.5 us (4%)
    all_gather x2, waiting for transfers between devices, operate(): piece = lax.all_gather(vector, 'row', axis=1, tiled=True)  54.5 us
    reduce_scatter x2, waiting for transfers between devices, operate(): lax.psum_scatter(partial_rows, 'col', scatter_dimension=1, tiled=True)  40.8 us
    psum x1, blocking collectives, body(): lax.psum((gram_of(precond, residual), gram_of(precond, product), gram_of(...  40.1 us
    psum x1, blocking collectives, global_sum(): return lax.psum((terms[0], terms[1]), ('row', 'col'))  39.2 us
    ppermute x4, waiting for transfers between devices, shifted(): return lax.ppermute(x, axis, pairs)  26.4 us
    another operation x9, other arithmetic, solve_spd(): factor = jnp.linalg.cholesky(matrix)  19.7 us
    another operation x6, other arithmetic, solve_spd(): return jax.scipy.linalg.cho_solve((factor, True), target)  18 us
    ppermute x4, starting transfers between devices, shifted(): return lax.ppermute(x, axis, pairs)  11.4 us
  transfers between devices with their start and end apart: 8, of which 8 were waited for; matrix products, arithmetic and copies ran while one was open for 7% of the time, Pallas kernels for 0%

commit v1 on v0

--- a/solution.py
+++ b/solution.py
@@ -58,7 +58,12 @@
         jnp.float32
     )
     initial = jnp.zeros((rhs_count, tile_rows * tile_len), jnp.float32)
-    piece = lax.all_gather(vector, "row", axis=1, tiled=True)
+    ring = [vector]
+    for hop in range(7):
+        ring.append(lax.ppermute(ring[-1], "row", [(dev, (dev + 1) % 8) for dev in range(8)]))
+    piece = jnp.roll(
+        jnp.concatenate(ring[::-1], axis=1), (lax.axis_index("row") + 1) * ring[0].shape[1], axis=1
+    )
     count_tiles = piece.shape[1] // tile_len
     pieces = piece.reshape(rhs_count, count_tiles, tile_len)
     coeffs = (

time: 341 us -> 379 us (1.11)
  waiting for transfers between devices: 122 us -> 160 us
    ppermute x0 -> x14, waiting for transfers between devices: none -> 90.8 us  [operate(): lax.ppermute(ring[-1], 'row', [(dev, (dev + 1) % 8) for dev in range(8)])]
    all_gather x2 -> x0, waiting for transfers between devices: 54.5 us -> none  [operate(): piece = lax.all_gather(vector, 'row', axis=1, tiled=True)]
    unnamed x42 -> x74, local copies, waits for them, and re-layouts: 10.7 us -> 11.7 us
  transfers between devices with their start and end apart: 8 -> 20, of which waited for: 8 -> 20; matrix products, arithmetic and copies ran while one was open for 7% -> 5% of each run, Pallas kernels for 0% -> 0%
where the time goes in v1:
time: 379 us; the launch traced here: 373 us
  waiting for transfers between devices  160 us (42%)
  blocking collectives  79.2 us (21%)
  matrix products  43.9 us (12%)
  other arithmetic  41 us (11%)
  local copies, waits for them, and re-layouts  19.2 us (5%)
  between operations  15.4 us (4%)
  starting transfers between devices  13.9 us (4%)
    ppermute x14, waiting for transfers between devices, operate(): lax.ppermute(ring[-1], 'row', [(dev, (dev + 1) % 8) for dev in range(8)])  90.8 us
    reduce_scatter x2, waiting for transfers between devices, operate(): lax.psum_scatter(partial_rows, 'col', scatter_dimension=1, tiled=True)  42.7 us
    psum x1, blocking collectives, body(): lax.psum((gram_of(precond, residual), gram_of(precond, product), gram_of(...  40 us
    psum x1, blocking collectives, global_sum(): return lax.psum((terms[0], terms[1]), ('row', 'col'))  39.2 us
    ppermute x4, waiting for transfers between devices, shifted(): return lax.ppermute(x, axis, pairs)  26.4 us
    another operation x9, other arithmetic, solve_spd(): factor = jnp.linalg.cholesky(matrix)  19.6 us
    another operation x6, other arithmetic, solve_spd(): return jax.scipy.linalg.cho_solve((factor, True), target)  17.9 us
    unnamed x74, local copies, waits for them, and re-layouts  11.7 us
  transfers between devices with their start and end apart: 20, of which 20 were waited for; matrix products, arithmetic and copies ran while one was open for 5% of the time, Pallas kernels for 0%

profile of v1, /device:TPU:0, one launch (start us, length us, event | category | flops | bytes accessed | tf_op | source)
XLA Modules:
  0.0 372.5 jit_solution(655319926039814902)
XLA Ops:
  7.2 5.0 %collective-permute-start = (f32[64,1024]{1,0:T(8,128)}, f32[64,1024]{1,0:T(8,128)S(1)}, u32[]{:S(2)}, u32[]{:S(2)}) collective-permute-start(f32[64,1024]{1,0:T(8,128)} %param.11), channel_id=1, source_target_pairs={{0,1},{1,2},{2,3},{3,4},{4,5},{5,6},{6,7},{7,8},{8,9},{9,10},{10,1... | collective-permute-start | bytes 786440 | tf_op jit(solution)/shard_map/ppermute | solution.py:13
  30.4 8.7 %collective-permute-done.1 = f32[64,1024]{1,0:T(8,128)S(1)} collective-permute-done((f32[64,1024]{1,0:T(8,128)S(1)}, f32[64,1024]{1,0:T(8,128)S(1)}, u32[]{:S(2)}, u32[]{:S(2)}) %collective-permute-start.1) | collective-permute-done | bytes 262176 | tf_op jit(solution)/shard_map/ppermute | solution.py:13
  40.5 7.1 %collective-permute-done.2 = f32[64,1024]{1,0:T(8,128)S(1)} collective-permute-done((f32[64,1024]{1,0:T(8,128)S(1)}, f32[64,1024]{1,0:T(8,128)S(1)}, u32[]{:S(2)}, u32[]{:S(2)}) %collective-permute-start.2) | collective-permute-done | bytes 262176 | tf_op jit(solution)/shard_map/ppermute | solution.py:63
  47.6 6.7 %collective-permute-done.3 = f32[64,1024]{1,0:T(8,128)S(1)} collective-permute-done((f32[64,1024]{1,0:T(8,128)S(1)}, f32[64,1024]{1,0:T(8,128)S(1)}, u32[]{:S(2)}, u32[]{:S(2)}) %collective-permute-start.3) | collective-permute-done | bytes 262176 | tf_op jit(solution)/shard_map/ppermute | solution.py:63
  54.3 6.7 %collective-permute-done.4 = f32[64,1024]{1,0:T(8,128)S(1)} collective-permute-done((f32[64,1024]{1,0:T(8,128)S(1)}, f32[64,1024]{1,0:T(8,128)S(1)}, u32[]{:S(2)}, u32[]{:S(2)}) %collective-permute-start.4) | collective-permute-done | bytes 262176 | tf_op jit(solution)/shard_map/ppermute | solution.py:63
  61.0 6.7 %collective-permute-done.5 = f32[64,1024]{1,0:T(8,128)S(1)} collective-permute-done((f32[64,1024]{1,0:T(8,128)S(1)}, f32[64,1024]{1,0:T(8,128)S(1)}, u32[]{:S(2)}, u32[]{:S(2)}) %collective-permute-start.5) | collective-permute-done | bytes 262176 | tf_op jit(solution)/shard_map/ppermute | solution.py:63
  67.7 6.7 %collective-permute-done.6 = f32[64,1024]{1,0:T(8,128)S(1)} collective-permute-done((f32[64,1024]{1,0:T(8,128)S(1)}, f32[64,1024]{1,0:T(8,128)S(1)}, u32[]{:S(2)}, u32[]{:S(2)}) %collective-permute-start.6) | collective-permute-done | bytes 262176 | tf_op jit(solution)/shard_map/ppermute | solution.py:63
  74.4 6.8 %collective-permute-done.7 = f32[64,1024]{1,0:T(8,128)} collective-permute-done((f32[64,1024]{1,0:T(8,128)S(1)}, f32[64,1024]{1,0:T(8,128)}, u32[]{:S(2)}, u32[]{:S(2)}) %collective-permute-start.7) | collective-permute-done | bytes 262176 | tf_op jit(solution)/shard_map/ppermute | solution.py:63
  102.2 27.1 %reduce-scatter.3.cloned.1.call-done = f32[64,1024]{1,0:T(8,128)} async-done(((f32[64,4096]{1,0:T(8,128)}), f32[64,1024]{1,0:T(8,128)}) %reduce-scatter.3.cloned.1.call-update) | async-done | bytes 262160 | tf_op jit(solution)/shard_map/reduce_scatter | solution.py:75
  135.2 39.2 %all-reduce.17 = (f32[64,64]{0,1:T(8,128)S(1)}, f32[64,64]{0,1:T(8,128)S(1)}) all-reduce(f32[64,64]{0,1:T(8,128)S(1)} %fusion.97, f32[64,64]{0,1:T(8,128)S(1)} %fusion.96), channel_id=1, replica_groups=mesh['row'=8,'col'=4] {'row','col'}, use_global_device_ids=true, to_apply=%region_6.9 | all-reduce | flops 8192 | bytes 65536 | tf_op jit(solution)/shard_map/psum | solution.py:93
  174.5 5.8 %cholesky.59 = f32[64,64]{1,0:T(8,128)S(1)} custom-call(f32[64,64]{1,0:T(8,128)S(1)} %fusion.89), custom_call_target="Cholesky" | custom-call | tf_op jit(solution)/shard_map/jit(cholesky)/cholesky | solution.py:80
  182.3 5.7 %custom-call.9 = f32[1,64,64]{1,2,0:T(8,128)S(1)} custom-call(f32[1,64,64]{2,1,0:T(8,128)} %fusion.72), custom_call_target="InvertDiagBlocksLowerTriangular" | custom-call | tf_op jit(solution)/shard_map/jit(_cho_solve)/triangular_solve | solution.py:81
  209.7 9.1 %collective-permute-done.10 = f32[64,1024]{1,0:T(8,128)S(1)} collective-permute-done((f32[64,1024]{1,0:T(8,128)S(1)}, f32[64,1024]{1,0:T(8,128)S(1)}, u32[]{:S(2)}, u32[]{:S(2)}) %collective-permute-start.10) | collective-permute-done | bytes 262176 | tf_op jit(solution)/shard_map/ppermute | solution.py:13
  218.9 6.7 %collective-permute-done.11 = f32[64,1024]{1,0:T(8,128)S(1)} collective-permute-done((f32[64,1024]{1,0:T(8,128)S(1)}, f32[64,1024]{1,0:T(8,128)S(1)}, u32[]{:S(2)}, u32[]{:S(2)}) %collective-permute-start.11) | collective-permute-done | bytes 262176 | tf_op jit(solution)/shard_map/ppermute | solution.py:63
  225.6 6.7 %collective-permute-done.12 = f32[64,1024]{1,0:T(8,128)S(1)} collective-permute-done((f32[64,1024]{1,0:T(8,128)S(1)}, f32[64,1024]{1,0:T(8,128)S(1)}, u32[]{:S(2)}, u32[]{:S(2)}) %collective-permute-start.12) | collective-permute-done | bytes 262176 | tf_op jit(solution)/shard_map/ppermute | solution.py:63
  232.3 6.7 %collective-permute-done.13 = f32[64,1024]{1,0:T(8,128)S(1)} collective-permute-done((f32[64,1024]{1,0:T(8,128)S(1)}, f32[64,1024]{1,0:T(8,128)S(1)}, u32[]{:S(2)}, u32[]{:S(2)}) %collective-permute-start.13) | collective-permute-done | bytes 262176 | tf_op jit(solution)/shard_map/ppermute | solution.py:63
  239.0 6.7 %collective-permute-done.14 = f32[64,1024]{1,0:T(8,128)S(1)} collective-permute-done((f32[64,1024]{1,0:T(8,128)S(1)}, f32[64,1024]{1,0:T(8,128)S(1)}, u32[]{:S(2)}, u32[]{:S(2)}) %collective-permute-start.14) | collective-permute-done | bytes 262176 | tf_op jit(solution)/shard_map/ppermute | solution.py:63
  245.7 6.7 %collective-permute-done.15 = f32[64,1024]{1,0:T(8,128)S(1)} collective-permute-done((f32[64,1024]{1,0:T(8,128)S(1)}, f32[64,1024]{1,0:T(8,128)S(1)}, u32[]{:S(2)}, u32[]{:S(2)}) %collective-permute-start.15) | collective-permute-done | bytes 262176 | tf_op jit(solution)/shard_map/ppermute | solution.py:63
  252.4 6.7 %collective-permute-done.16 = f32[64,1024]{1,0:T(8,128)S(1)} collective-permute-done((f32[64,1024]{1,0:T(8,128)S(1)}, f32[64,1024]{1,0:T(8,128)S(1)}, u32[]{:S(2)}, u32[]{:S(2)}) %collective-permute-start.16) | collective-permute-done | bytes 262176 | tf_op jit(solution)/shard_map/ppermute | solution.py:63
  259.3 6.7 %collective-permute-done.17 = f32[64,1024]{1,0:T(8,128)S(1)} collective-permute-done((f32[64,1024]{1,0:T(8,128)S(1)}, f32[64,1024]{1,0:T(8,128)S(1)}, u32[]{:S(2)}, u32[]{:S(2)}) %collective-permute-start.17) | collective-permute-done | bytes 262176 | tf_op jit(solution)/shard_map/ppermute | solution.py:63
  274.1 5.8 %cholesky.70 = f32[64,64]{1,0:T(8,128)S(1)} custom-call(f32[64,64]{1,0:T(8,128)S(1)} %fusion.84), custom_call_target="Cholesky" | custom-call | tf_op jit(solution)/shard_map/jit(cholesky)/cholesky | solution.py:80
  286.6 15.6 %reduce-scatter.5.cloned.1.call-done = f32[64,1024]{1,0:T(8,128)} async-done(((f32[64,4096]{1,0:T(8,128)}), f32[64,1024]{1,0:T(8,128)}) %reduce-scatter.5.cloned.1.call-update) | async-done | bytes 262160 | tf_op jit(solution)/shard_map/reduce_scatter | solution.py:75
  307.7 40.0 %all-reduce.16 = (f32[64,64]{1,0:T(8,128)S(1)}, f32[64,64]{1,0:T(8,128)S(1)}, f32[64,64]{0,1:T(8,128)S(1)}) all-reduce(f32[64,64]{1,0:T(8,128)S(1)} %fusion.100, f32[64,64]{1,0:T(8,128)S(1)} %fusion.99, f32[64,64]{0,1:T(8,128)S(1)} %fusion.98), channel_id=1, replica_groups=mesh['row'=8,'col'=4] {'row','col'}, use_global_device_ids=true, to_apply=%region_10.14 | all-reduce | flops 12288 | bytes 98304 | tf_op jit(solution)/shard_map/psum | solution.py:107
  350.1 5.8 %cholesky.81 = f32[64,64]{1,0:T(8,128)S(1)} custom-call(f32[64,64]{1,0:T(8,128)S(1)} %fusion.79), custom_call_target="Cholesky" | custom-call | tf_op jit(solution)/shard_map/jit(cholesky)/cholesky | solution.py:80
  (177 shorter events, 101.8 us)
Async XLA Ops:
  7.2 122.1 %reduce-scatter.3.cloned.1.call-start = ((), (), s32[]{:S(2)}) async-start(), calls=%async_computation.2 | async-start | bytes 1310720 | tf_op jit(solution)/shard_map/reduce_scatter | solution.py:75
  7.2 10.8 %collective-permute-start = (f32[64,1024]{1,0:T(8,128)}, f32[64,1024]{1,0:T(8,128)S(1)}, u32[]{:S(2)}, u32[]{:S(2)}) collective-permute-start(f32[64,1024]{1,0:T(8,128)} %param.11), channel_id=1, source_target_pairs={{0,1},{1,2},{2,3},{3,4},{4,5},{5,6},{6,7},{7,8},{8,9},{9,10},{10,1... | collective-permute-start | bytes 786440 | tf_op jit(solution)/shard_map/ppermute | solution.py:13
  28.7 53.0 %copy-start.8 = (f32[4,1,8,2,12,1024]{5,3,4,2,1,0:T(2,128)S(1)}, f32[4,1,8,2,12,1024]{5,3,4,2,1,0:T(2,128)}, u32[]{:S(2)}) copy-start(f32[4,1,8,2,12,1024]{5,3,4,2,1,0:T(2,128)} %param.13) | copy-start | bytes 9437188
  29.0 10.1 %collective-permute-start.1 = (f32[64,1024]{1,0:T(8,128)S(1)}, f32[64,1024]{1,0:T(8,128)S(1)}, u32[]{:S(2)}, u32[]{:S(2)}) collective-permute-start(f32[64,1024]{1,0:T(8,128)S(1)} %bitcast.318), channel_id=1, source_target_pairs={{1,0},{2,1},{3,2},{4,3},{5,4},{6,5},{7,6},{8,7},{9,8},{10,9},{11,1... | collective-permute-start | bytes 786440 | tf_op jit(solution)/shard_map/ppermute | solution.py:13
  39.2 46.1 %copy-start.19 = (s32[4,1,8]{2,1,0:T(1,128)S(1)}, s32[4,1,8]{2,1,0:T(1,128)}, u32[]{:S(2)}) copy-start(s32[4,1,8]{2,1,0:T(1,128)} %param.14) | copy-start | bytes 388
  39.2 8.4 %collective-permute-start.2 = (f32[64,1024]{1,0:T(8,128)S(1)}, f32[64,1024]{1,0:T(8,128)S(1)}, u32[]{:S(2)}, u32[]{:S(2)}) collective-permute-start(f32[64,1024]{1,0:T(8,128)S(1)} %bitcast_add_fusion.1), channel_id=1, source_target_pairs={{0,4},{4,8},{8,12},{12,16},{16,20},{20,24},{24,28},{28,0},{1,5},{5... | collective-permute-start | bytes 786440 | tf_op jit(solution)/shard_map/ppermute | solution.py:63
  47.6 6.7 %collective-permute-start.3 = (f32[64,1024]{1,0:T(8,128)S(1)}, f32[64,1024]{1,0:T(8,128)S(1)}, u32[]{:S(2)}, u32[]{:S(2)}) collective-permute-start(f32[64,1024]{1,0:T(8,128)S(1)} %collective-permute-done.2), channel_id=1, source_target_pairs={{0,4},{4,8},{8,12},{12,16},{16,20},{20,24},{24,28},{28,0},{1,5},{5... | collective-permute-start | bytes 786440 | tf_op jit(solution)/shard_map/ppermute | solution.py:63
  54.3 6.7 %collective-permute-start.4 = (f32[64,1024]{1,0:T(8,128)S(1)}, f32[64,1024]{1,0:T(8,128)S(1)}, u32[]{:S(2)}, u32[]{:S(2)}) collective-permute-start(f32[64,1024]{1,0:T(8,128)S(1)} %collective-permute-done.3), channel_id=1, source_target_pairs={{0,4},{4,8},{8,12},{12,16},{16,20},{20,24},{24,28},{28,0},{1,5},{5... | collective-permute-start | bytes 786440 | tf_op jit(solution)/shard_map/ppermute | solution.py:63
  61.0 6.7 %collective-permute-start.5 = (f32[64,1024]{1,0:T(8,128)S(1)}, f32[64,1024]{1,0:T(8,128)S(1)}, u32[]{:S(2)}, u32[]{:S(2)}) collective-permute-start(f32[64,1024]{1,0:T(8,128)S(1)} %collective-permute-done.4), channel_id=1, source_target_pairs={{0,4},{4,8},{8,12},{12,16},{16,20},{20,24},{24,28},{28,0},{1,5},{5... | collective-permute-start | bytes 786440 | tf_op jit(solution)/shard_map/ppermute | solution.py:63
  67.7 6.7 %collective-permute-start.6 = (f32[64,1024]{1,0:T(8,128)S(1)}, f32[64,1024]{1,0:T(8,128)S(1)}, u32[]{:S(2)}, u32[]{:S(2)}) collective-permute-start(f32[64,1024]{1,0:T(8,128)S(1)} %collective-permute-done.5), channel_id=1, source_target_pairs={{0,4},{4,8},{8,12},{12,16},{16,20},{20,24},{24,28},{28,0},{1,5},{5... | collective-permute-start | bytes 786440 | tf_op jit(solution)/shard_map/ppermute | solution.py:63
  74.4 6.8 %collective-permute-start.7 = (f32[64,1024]{1,0:T(8,128)S(1)}, f32[64,1024]{1,0:T(8,128)}, u32[]{:S(2)}, u32[]{:S(2)}) collective-permute-start(f32[64,1024]{1,0:T(8,128)S(1)} %collective-permute-done.6), channel_id=1, source_target_pairs={{0,4},{4,8},{8,12},{12,16},{16,20},{20,24},{24,28},{28,0},{1,5},{5... | collective-permute-start | bytes 786440 | tf_op jit(solution)/shard_map/ppermute | solution.py:63
  81.2 7.6 %collective-permute-start.8 = (f32[64,1024]{1,0:T(8,128)}, f32[64,1024]{1,0:T(8,128)}, u32[]{:S(2)}, u32[]{:S(2)}) collective-permute-start(f32[64,1024]{1,0:T(8,128)} %collective-permute-done.7), channel_id=1, source_target_pairs={{0,4},{4,8},{8,12},{12,16},{16,20},{20,24},{24,28},{28,0},{1,5},{5... | collective-permute-start | bytes 786440 | tf_op jit(solution)/shard_map/ppermute | solution.py:63
  100.6 201.5 %reduce-scatter.5.cloned.1.call-start = ((), (), s32[]{:S(2)}) async-start(), calls=%async_computation.3 | async-start | bytes 1310720 | tf_op jit(solution)/shard_map/reduce_scatter | solution.py:75
  189.9 8.5 %collective-permute-start.9 = (f32[64,1024]{1,0:T(8,128)S(1)}, f32[64,1024]{1,0:T(8,128)S(1)}, u32[]{:S(2)}, u32[]{:S(2)}) collective-permute-start(f32[64,1024]{1,0:T(8,128)S(1)} %convolution_subtract_fusion.1), channel_id=1, source_target_pairs={{0,1},{1,2},{2,3},{3,4},{4,5},{5,6},{6,7},{7,8},{8,9},{9,10},{10,1... | collective-permute-start | bytes 786440 | tf_op jit(solution)/shard_map/ppermute | solution.py:13
  208.4 10.4 %collective-permute-start.10 = (f32[64,1024]{1,0:T(8,128)S(1)}, f32[64,1024]{1,0:T(8,128)S(1)}, u32[]{:S(2)}, u32[]{:S(2)}) collective-permute-start(f32[64,1024]{1,0:T(8,128)S(1)} %bitcast.319), channel_id=1, source_target_pairs={{1,0},{2,1},{3,2},{4,3},{5,4},{6,5},{7,6},{8,7},{9,8},{10,9},{11,1... | collective-permute-start | bytes 786440 | tf_op jit(solution)/shard_map/ppermute | solution.py:13
  218.8 47.3 %copy-start.2 = (f32[64,1024]{1,0:T(8,128)}, f32[64,1024]{1,0:T(8,128)S(1)}, u32[]{:S(2)}) copy-start(f32[64,1024]{1,0:T(8,128)S(1)} %bitcast_add_fusion) | copy-start | bytes 786436
  218.8 6.7 %collective-permute-start.11 = (f32[64,1024]{1,0:T(8,128)S(1)}, f32[64,1024]{1,0:T(8,128)S(1)}, u32[]{:S(2)}, u32[]{:S(2)}) collective-permute-start(f32[64,1024]{1,0:T(8,128)S(1)} %bitcast_add_fusion), channel_id=1, source_target_pairs={{0,4},{4,8},{8,12},{12,16},{16,20},{20,24},{24,28},{28,0},{1,5},{5... | collective-permute-start | bytes 786440 | tf_op jit(solution)/shard_map/ppermute | solution.py:63
  225.6 6.7 %collective-permute-start.12 = (f32[64,1024]{1,0:T(8,128)S(1)}, f32[64,1024]{1,0:T(8,128)S(1)}, u32[]{:S(2)}, u32[]{:S(2)}) collective-permute-start(f32[64,1024]{1,0:T(8,128)S(1)} %collective-permute-done.11), channel_id=1, source_target_pairs={{0,4},{4,8},{8,12},{12,16},{16,20},{20,24},{24,28},{28,0},{1,5},{5... | collective-permute-start | bytes 786440 | tf_op jit(solution)/shard_map/ppermute | solution.py:63
  232.3 6.7 %collective-permute-start.13 = (f32[64,1024]{1,0:T(8,128)S(1)}, f32[64,1024]{1,0:T(8,128)S(1)}, u32[]{:S(2)}, u32[]{:S(2)}) collective-permute-start(f32[64,1024]{1,0:T(8,128)S(1)} %collective-permute-done.12), channel_id=1, source_target_pairs={{0,4},{4,8},{8,12},{12,16},{16,20},{20,24},{24,28},{28,0},{1,5},{5... | collective-permute-start | bytes 786440 | tf_op jit(solution)/shard_map/ppermute | solution.py:63
  239.0 6.7 %collective-permute-start.14 = (f32[64,1024]{1,0:T(8,128)S(1)}, f32[64,1024]{1,0:T(8,128)S(1)}, u32[]{:S(2)}, u32[]{:S(2)}) collective-permute-start(f32[64,1024]{1,0:T(8,128)S(1)} %collective-permute-done.13), channel_id=1, source_target_pairs={{0,4},{4,8},{8,12},{12,16},{16,20},{20,24},{24,28},{28,0},{1,5},{5... | collective-permute-start | bytes 786440 | tf_op jit(solution)/shard_map/ppermute | solution.py:63
  245.7 6.7 %collective-permute-start.15 = (f32[64,1024]{1,0:T(8,128)S(1)}, f32[64,1024]{1,0:T(8,128)S(1)}, u32[]{:S(2)}, u32[]{:S(2)}) collective-permute-start(f32[64,1024]{1,0:T(8,128)S(1)} %collective-permute-done.14), channel_id=1, source_target_pairs={{0,4},{4,8},{8,12},{12,16},{16,20},{20,24},{24,28},{28,0},{1,5},{5... | collective-permute-start | bytes 786440 | tf_op jit(solution)/shard_map/ppermute | solution.py:63
  252.4 6.7 %collective-permute-start.16 = (f32[64,1024]{1,0:T(8,128)S(1)}, f32[64,1024]{1,0:T(8,128)S(1)}, u32[]{:S(2)}, u32[]{:S(2)}) collective-permute-start(f32[64,1024]{1,0:T(8,128)S(1)} %collective-permute-done.15), channel_id=1, source_target_pairs={{0,4},{4,8},{8,12},{12,16},{16,20},{20,24},{24,28},{28,0},{1,5},{5... | collective-permute-start | bytes 786440 | tf_op jit(solution)/shard_map/ppermute | solution.py:63
  259.1 6.9 %collective-permute-start.17 = (f32[64,1024]{1,0:T(8,128)S(1)}, f32[64,1024]{1,0:T(8,128)S(1)}, u32[]{:S(2)}, u32[]{:S(2)}) collective-permute-start(f32[64,1024]{1,0:T(8,128)S(1)} %collective-permute-done.16), channel_id=1, source_target_pairs={{0,4},{4,8},{8,12},{12,16},{16,20},{20,24},{24,28},{28,0},{1,5},{5... | collective-permute-start | bytes 786440 | tf_op jit(solution)/shard_map/ppermute | solution.py:63
  286.6 61.6 %copy-start.5 = (f32[64,1024]{1,0:T(8,128)S(1)}, f32[64,1024]{1,0:T(8,128)}, u32[]{:S(2)}) copy-start(f32[64,1024]{1,0:T(8,128)} %copy-done.4) | copy-start | bytes 786436
  (16 other events, 177.2 us)
Sparse Core Ops, SparseCore 0:
  100.8 28.4 reduce-scatter.2
  274.2 27.9 reduce-scatter.4
